TPU v7x, 32 devices: a whole 2x2x4 slice. The times are simulated.
32 devices in a mesh: surf: 8 (over z, x), col: 4 (over y, core).
Axes of the slice: x: 2, y: 2, z: 4, core: 2. Of those that a mesh axis runs over, the one named last changes fastest.
Arguments:
- stiffness: float32 [32, 3, 512, 512], P(('surf', 'col'))
- load: float32 [32, 3, 512, 256], P(('surf', 'col')), may hold values from -6 to 6
- start: float32 [32, 3, 512, 256], P(('surf', 'col')), may hold values from -6 to 6
- boundary_matrix: float32 [512, 4, 2048], P('surf', None, 'col'), may hold values from -0.125 to 0.125
- bem_node: int32 [4, 512], P('col'), may hold values from 0 to 511, as said below
Outputs:
- solution_field: float32 [32, 3, 512, 256], P(('surf', 'col'))
- traction: float32 [4, 512, 256], P('col', 'surf')
Inputs may be any that keep to these rules, and one draw needn't show every extreme that they name: Each row bem_node[g] is a permutation of 0 to 512 - 1 (the top face nodes of column group g). For each block of 64 slots q in [s * 64, (s + 1) * 64) and each patch s2 of the group, the block's slots name either exactly 8 node of patch s2 or none; each patch's top face nodes lie in exactly 8 blocks.
All inputs are finite; a program needn't handle non-finite values.
Results may differ from a plain program's by a relative error of at most 0.0001.
Values sent between devices are 32-bit elements; how exact they have to be, the bound alone decides.
No kernel may reach another device: no remote copies, remote signals or barrier semaphores. Data moves between devices by JAX's collectives and lax.ppermute only.
A program may use at most 128 MiB of HBM per device.

v0:
```python
import jax
import jax.numpy as jnp
from jax import lax
from jax.sharding import PartitionSpec as P

EDGE = 8
ITERS = 2
damping = 0.25
coupling = 0.5


def with_halo(block, sides, width):
    for axis, dim in sides:
        count = lax.axis_size(axis)
        forward = [(i, i + 1) for i in range(count - 1)]
        backward = [(target, source) for source, target in forward]
        low = lax.ppermute(
            lax.slice_in_dim(block, block.shape[dim] - width, None, axis=dim), axis, forward
        )
        high = lax.ppermute(lax.slice_in_dim(block, 0, width, axis=dim), axis, backward)
        block = jnp.concatenate([low, block, high], axis=dim)
    return block


def volume_apply(current, kmats, edge_cells, layers_deep, fields):
    highest = lax.Precision.HIGHEST
    cube = current.reshape(layers_deep, edge_cells, edge_cells, edge_cells, fields)
    padded = with_halo(cube, (("surf", 1), ("col", 2)), 1)
    extra = jnp.zeros_like(cube)
    extra = extra.at[:, 0].add(cube[:, 0] - padded[:, 0, 1:-1])
    extra = extra.at[:, -1].add(cube[:, -1] - padded[:, -1, 1:-1])
    extra = extra.at[:, :, 0].add(cube[:, :, 0] - padded[:, 1:-1, 0])
    extra = extra.at[:, :, -1].add(cube[:, :, -1] - padded[:, 1:-1, -1])
    low_k = cube[:, :, :, 0]
    high_k = cube[:, :, :, -1]
    deeper = jnp.concatenate([low_k[1:], jnp.zeros_like(low_k[:1])], axis=0)
    extra = extra.at[:, :, :, -1].add(high_k - deeper)
    extra = extra.at[1:, :, :, 0].add(low_k[1:] - high_k[:-1])
    applied = jnp.einsum("dab,dbf->daf", kmats, current, precision=highest)
    return applied.reshape(cube.shape) + coupling * extra


def rank_within(labels_row, order_key):
    same_label = labels_row[:, None] == labels_row[None, :]
    earlier = order_key[None, :] < order_key[:, None]
    return jnp.sum(jnp.logical_and(same_label, earlier), axis=1)


def shards(stiffness, load, start, boundary_matrix, bem_node):
    highest = lax.Precision.HIGHEST
    surf_count = lax.axis_size("surf")
    my_index = lax.axis_index("surf")
    layers_deep = stiffness.shape[1]
    node_count = stiffness.shape[2]
    fields = load.shape[3]
    edge_cells = EDGE
    face_nodes = edge_cells * edge_cells
    per_pair = max(face_nodes // surf_count, 1)
    group_map = bem_node[0]
    group_size = group_map.shape[0]
    slot_of_node = jnp.argsort(group_map)
    kmats = stiffness[0]
    load_cube = load[0].reshape(layers_deep, edge_cells, edge_cells, edge_cells, fields)
    operator_rows = boundary_matrix.reshape(-1, group_size)
    local_order = jnp.arange(face_nodes, dtype=jnp.int32)
    my_block_nodes = lax.dynamic_slice_in_dim(group_map, my_index * face_nodes, face_nodes)
    block_owners = my_block_nodes // face_nodes
    block_local = my_block_nodes % face_nodes
    slot_index = block_owners * per_pair + rank_within(block_owners, block_local)
    my_node_slots = lax.dynamic_slice_in_dim(slot_of_node, my_index * face_nodes, face_nodes)
    node_holders = my_node_slots // face_nodes
    send_index = node_holders * per_pair + rank_within(node_holders, local_order)
    current = start[0]
    traction_rows = jnp.zeros((face_nodes, fields), jnp.float32)
    for turn_index in range(ITERS):
        cube = current.reshape(layers_deep, edge_cells, edge_cells, edge_cells, fields)
        top_face = cube[0, :, :, 0, :].reshape(face_nodes, fields)
        gathered = lax.all_gather(top_face, "surf", axis=0, tiled=True)
        ordered = jnp.take(gathered, group_map, axis=0)
        partial_value = jnp.dot(
            operator_rows, ordered, precision=highest, preferred_element_type=jnp.float32
        )
        summed = lax.psum_scatter(
            partial_value.reshape(face_nodes, -1, fields), "col", scatter_dimension=1, tiled=True
        )
        traction_rows = summed.reshape(face_nodes, fields)
        outgoing_back = (
            jnp.zeros((surf_count * per_pair, fields), jnp.float32)
            .at[slot_index]
            .set(traction_rows)
        )
        returned = lax.all_to_all(
            outgoing_back.reshape(surf_count, per_pair, fields),
            "surf",
            split_axis=0,
            concat_axis=0,
            tiled=True,
        )
        on_top = jnp.take(returned.reshape(surf_count * per_pair, fields), send_index, axis=0)
        applied = volume_apply(current, kmats, edge_cells, layers_deep, fields)
        applied = applied.at[0, :, :, 0, :].add(on_top.reshape(edge_cells, edge_cells, fields))
        residual = load_cube - applied
        current = (cube + damping * residual).reshape(layers_deep, node_count, fields)
    return (current[None], traction_rows[None])


def solution(mesh):
    in_specs = (
        P(("surf", "col"), None, None, None),
        P(("surf", "col"), None, None, None),
        P(("surf", "col"), None, None, None),
        P("surf", None, "col"),
        P("col", None),
    )
    out_specs = (P(("surf", "col"), None, None, None), P("col", "surf", None))
    return jax.shard_map(shards, mesh=mesh, in_specs=in_specs, out_specs=out_specs, check_vma=False)
```

profile of v0, /device:TPU:1, one launch (start us, length us, event | category | flops | bytes accessed | tf_op | source)
XLA Modules:
  0.0 254.0 jit_solution(10524862129218521562)
XLA Ops:
  7.2 2.1 copy.71
  9.3 1.2 copy-done.5
  11.2 4.6 %collective-permute-start = (f32[3,1,8,8,256]{4,2,1,0,3:T(8,128)}, f32[3,1,8,8,256]{4,2,1,0,3:T(8,128)}, u32[]{:S(2)}, u32[]{:S(2)}) collective-permute-start(f32[3,1,8,8,256]{4,2,1,0,3:T(8,128)} %slice.588), channel_id=1, source_target_pairs={{0,4},{4,8},{8,12},{12,16},{16,20},{20,24},{24,28},{1,5},{5,9},{9,... | collective-permute-start | bytes 589832 | tf_op jit(solution)/shard_map/ppermute | solution.py:17
  15.8 1.1 slice.603
  16.9 28.2 %all_gather.6 = f32[512,256]{1,0:T(8,128)} all-gather(f32[64,256]{1,0:T(8,128)S(1)} %bitcast.136), channel_id=1, replica_groups=mesh['surf'=8,'col'=4] {'surf'}, dimensions={0}, use_global_device_ids=true | all-gather | bytes 589824 | tf_op jit(solution)/shard_map/all_gather | solution.py:78
  45.2 2.0 reshape.729
  47.2 3.3 %gather_fusion = f32[512,256]{1,0:T(8,128)} fusion(f32[512,256]{1,0:T(8,128)} %all_gather.6, s32[1024]{0:T(1024)S(1)} %pad_clamp_fusion.1), kind=kCustom, calls=%fused_computation.clone | custom fusion | bytes 1050624 | tf_op jit(solution)/shard_map/jit(_take)/gather | solution.py:79
  50.5 1.9 convolution_bitcast_fusion.1
  53.2 1.7 copy.79
  54.9 5.4 %fusion.2 = f32[3,512,256]{2,1,0:T(8,128)} fusion(f32[1,3,512,512]{3,2,1,0:T(8,128)S(1)} %copy-done, f32[1,3,512,256]{3,2,1,0:T(8,128)} %param.39), kind=kOutput, calls=%fused_computation.8 | convolution fusion | flops 2415919104 | bytes 6291456 | tf_op jit(solution)/shard_map/dab,dbf->daf/dot_general | solution.py:39
  60.4 3.8 %sort.17 = (s32[512]{0:T(512)}, s32[512]{0:T(512)S(1)}) sort(s32[512]{0:T(512)S(1)} %bitcast.141, s32[512]{0:T(512)S(1)} %iota.11), dimensions={0}, to_apply=%region_3.5 | sort | flops 4608 | bytes 8192 | tf_op jit(solution)/shard_map/jit(argsort)/sort | solution.py:61
  64.6 1.1 fusion.44
  65.8 1.3 collective-permute-start.1
  67.1 1.3 scatter-add.46
  68.8 3.3 %collective-permute-done.1 = f32[3,1,8,8,256]{4,2,1,0,3:T(8,128)S(1)} collective-permute-done((f32[3,1,8,8,256]{4,2,1,0,3:T(8,128)S(1)}, f32[3,1,8,8,256]{4,2,1,0,3:T(8,128)S(1)}, u32[]{:S(2)}, u32[]{:S(2)}) %collective-permute-start.1) | collective-permute-done | bytes 196640 | tf_op jit(solution)/shard_map/ppermute | solution.py:20
  72.2 1.7 constant_dynamic-update-slice_fusion
  73.9 1.1 fusion.41
  74.9 10.4 %collective-permute-start.2 = (f32[3,10,1,8,256]{4,2,1,0,3:T(1,128)}, f32[3,10,1,8,256]{4,2,1,0,3:T(1,128)}, u32[]{:S(2)}, u32[]{:S(2)}) collective-permute-start(f32[3,10,1,8,256]{4,2,1,0,3:T(1,128)} %get-tuple-element.181), channel_id=1, source_target_pairs={{0,1},{1,2},{2,3},{4,5},{5,6},{6,7},{8,9},{9,10},{10,11},{12,13},{... | collective-permute-start | bytes 737288 | tf_op jit(solution)/shard_map/ppermute | solution.py:17
  85.5 1.9 collective-permute-start.3
  87.4 1.7 scatter_custom_fusion
  89.1 3.4 %all-to-all-start = ((f32[8,8,256]{2,1,0:T(8,128)}), f32[8,8,256]{2,1,0:T(8,128)S(1)}, u32[]{:S(2)}, u32[]{:S(2)}) async-start(f32[8,8,256]{2,1,0:T(8,128)} %bitcast.16), calls=%async_computation.1 | async-start | bytes 131072 | tf_op jit(solution)/shard_map/all_to_all | solution.py:92
  92.7 2.3 fusion.25
  95.0 4.5 %scatter-add.50 = f32[3,8,8,8,256]{4,2,1,0,3:T(8,128)} dynamic-update-slice(f32[3,8,8,8,256]{4,2,1,0,3:T(8,128)} %get-tuple-element.193, f32[3,8,1,8,256]{4,2,1,0,3:T(1,128)S(1)} %fusion.25, s32[]{:T(128)} %constant.397.clone.1, s32[]{:T(128)} %constant.397.clone.1, s32[]{:T(128)} %constant.397.clone.1, s32[]{:T(128)} %constant.397.clone.1, s32[]{:T(128)} %constant.397.clone.1) | dynamic-update-slice | bytes 393220 | tf_op jit(solution)/shard_map/scatter-add | solution.py:32
  99.5 2.4 fusion.24
  101.9 4.5 %scatter-add.51 = f32[3,8,8,8,256]{4,2,1,0,3:T(8,128)} dynamic-update-slice(f32[3,8,8,8,256]{4,2,1,0,3:T(8,128)} %scatter-add.50, f32[3,8,1,8,256]{4,2,1,0,3:T(1,128)S(1)} %fusion.24, s32[]{:T(128)} %constant.397.clone.1, s32[]{:T(128)} %constant.397.clone.1, s32[]{:T(128)} %constant.398.clone.1, s32[]{:T(128)} %constant.397.clone.1, s32[]{:T(128)} %constant.397.clone.1) | dynamic-update-slice | bytes 393220 | tf_op jit(solution)/shard_map/scatter-add | solution.py:33
  106.4 1.7 fusion.23
  108.1 3.5 %copy.78 = f32[3,8,8,8,256]{4,3,2,1,0:T(8,128)} copy(f32[3,8,8,8,256]{4,2,1,0,3:T(8,128)} %fusion.23) | data formatting | bytes 3145728 | tf_op jit(solution)/shard_map/scatter-add | solution.py:37
  112.5 1.8 fusion.27
  114.3 4.0 %scatter-add.55 = f32[3,8,8,8,256]{4,3,2,1,0:T(8,128)} dynamic-update-slice(f32[3,8,8,8,256]{4,3,2,1,0:T(8,128)} %copy.78, f32[2,8,8,1,256]{4,3,2,1,0:T(1,128)S(1)} %fusion.27, s32[]{:T(128)} %constant.399.clone.1, s32[]{:T(128)} %constant.397.clone.1, s32[]{:T(128)} %constant.397.clone.1, s32[]{:T(128)} %constant.397.clone.1, s32[]{:T(128)} %constant.397.clone.1) | dynamic-update-slice | bytes 262148 | tf_op jit(solution)/shard_map/scatter-add | solution.py:38
  118.3 3.3 %multiply_add_fusion.3 = f32[3,8,8,8,256]{4,3,2,1,0:T(8,128)} fusion(f32[3,8,8,8,256]{4,3,2,1,0:T(8,128)} %bitcast.130, f32[3,8,8,8,256]{4,3,2,1,0:T(8,128)} %scatter-add.55), kind=kLoop, calls=%fused_computation.14 | loop fusion | flops 786432 | bytes 4718592 | tf_op jit(solution)/shard_map/add | solution.py:40
  122.3 1.1 slice_add_fusion.1
  123.5 2.3 scatter-add.56
  125.8 2.8 %multiply_add_fusion.2 = f32[3,8,8,8,256]{4,3,2,1,0:T(8,128)S(1)} fusion(f32[3,8,8,8,256]{4,3,2,1,0:T(8,128)} %bitcast.124, f32[3,8,8,8,256]{4,3,2,1,0:T(8,128)} %bitcast.128, f32[3,8,8,8,256]{4,3,2,1,0:T(8,128)} %scatter-add.56), kind=kLoop, calls=%fused_computation.13 | loop fusion | flops 1179648 | bytes 6291456 | tf_op jit(solution)/shard_map/add | solution.py:103
  129.7 1.1 copy-done.6
  131.6 3.7 %collective-permute-start.4 = (f32[3,1,8,8,256]{4,2,1,0,3:T(8,128)}, f32[3,1,8,8,256]{4,2,1,0,3:T(8,128)}, u32[]{:S(2)}, u32[]{:S(2)}) collective-permute-start(f32[3,1,8,8,256]{4,2,1,0,3:T(8,128)} %slice.605), channel_id=1, source_target_pairs={{0,4},{4,8},{8,12},{12,16},{16,20},{20,24},{24,28},{1,5},{5,9},{9,... | collective-permute-start | bytes 589832 | tf_op jit(solution)/shard_map/ppermute | solution.py:17
  135.3 28.4 %all_gather.7 = f32[512,256]{1,0:T(8,128)} all-gather(f32[64,256]{1,0:T(8,128)S(1)} %bitcast.137), channel_id=1, replica_groups=mesh['surf'=8,'col'=4] {'surf'}, dimensions={0}, use_global_device_ids=true | all-gather | bytes 589824 | tf_op jit(solution)/shard_map/all_gather | solution.py:78
  163.7 3.3 %gather_fusion.2 = f32[512,256]{1,0:T(8,128)} fusion(f32[512,256]{1,0:T(8,128)} %all_gather.7, s32[1024]{0:T(1024)S(1)} %pad_clamp_fusion.1), kind=kCustom, calls=%fused_computation.2.clone | custom fusion | bytes 1050624 | tf_op jit(solution)/shard_map/jit(_take)/gather | solution.py:79
  167.0 1.9 convolution_bitcast_fusion
  169.7 1.7 copy.91
  171.4 1.2 fusion.43
  172.6 1.4 scatter-add.59
  174.0 1.3 collective-permute-start.5
  175.8 4.6 %collective-permute-done.5 = f32[3,1,8,8,256]{4,2,1,0,3:T(8,128)S(1)} collective-permute-done((f32[3,1,8,8,256]{4,2,1,0,3:T(8,128)S(1)}, f32[3,1,8,8,256]{4,2,1,0,3:T(8,128)S(1)}, u32[]{:S(2)}, u32[]{:S(2)}) %collective-permute-start.5) | collective-permute-done | bytes 196640 | tf_op jit(solution)/shard_map/ppermute | solution.py:20
  180.4 1.7 constant_dynamic-update-slice_fusion.3
  182.1 1.1 fusion.40
  183.2 10.5 %collective-permute-start.6 = (f32[3,10,1,8,256]{4,2,1,0,3:T(1,128)}, f32[3,10,1,8,256]{4,2,1,0,3:T(1,128)}, u32[]{:S(2)}, u32[]{:S(2)}) collective-permute-start(f32[3,10,1,8,256]{4,2,1,0,3:T(1,128)} %get-tuple-element.179), channel_id=1, source_target_pairs={{0,1},{1,2},{2,3},{4,5},{5,6},{6,7},{8,9},{9,10},{10,11},{12,13},{... | collective-permute-start | bytes 737288 | tf_op jit(solution)/shard_map/ppermute | solution.py:17
  193.7 6.5 %fusion.5 = f32[3,512,256]{1,2,0:T(8,128)} fusion(f32[3,512,256]{2,1,0:T(8,128)S(1)} %bitcast.120, f32[1,3,512,512]{3,2,1,0:T(8,128)S(1)} %copy-done), kind=kOutput, calls=%fused_computation.15 | convolution fusion | flops 2415919104 | bytes 6291456 | tf_op jit(solution)/shard_map/dab,dbf->daf/dot_general | solution.py:39
  200.3 3.0 %copy.82 = f32[3,512,256]{2,1,0:T(8,128)} copy(f32[3,512,256]{1,2,0:T(8,128)} %fusion.5) | data formatting | bytes 3145728 | tf_op jit(solution)/shard_map/dab,dbf->daf/dot_general | solution.py:39
  203.3 1.8 fusion.42
  205.1 1.9 collective-permute-start.7
  207.1 1.7 scatter_custom_fusion.1
  208.8 3.3 %all-to-all-start.1 = ((f32[8,8,256]{2,1,0:T(8,128)}), f32[8,8,256]{2,1,0:T(8,128)S(1)}, u32[]{:S(2)}, u32[]{:S(2)}) async-start(f32[8,8,256]{2,1,0:T(8,128)} %bitcast.26), calls=%async_computation.3 | async-start | bytes 131072 | tf_op jit(solution)/shard_map/all_to_all | solution.py:92
  212.1 1.8 fusion.19
  214.0 4.5 %scatter-add.61 = f32[3,8,8,8,256]{4,2,1,0,3:T(8,128)} dynamic-update-slice(f32[3,8,8,8,256]{4,2,1,0,3:T(8,128)} %get-tuple-element.191, f32[3,8,1,8,256]{4,2,1,0,3:T(1,128)S(1)} %fusion.19, s32[]{:T(128)} %constant.397.clone.1, s32[]{:T(128)} %constant.397.clone.1, s32[]{:T(128)} %constant.397.clone.1, s32[]{:T(128)} %constant.397.clone.1, s32[]{:T(128)} %constant.397.clone.1) | dynamic-update-slice | bytes 393220 | tf_op jit(solution)/shard_map/scatter-add | solution.py:32
  218.5 1.9 fusion.18
  220.4 4.5 %scatter-add.64 = f32[3,8,8,8,256]{4,2,1,0,3:T(8,128)} dynamic-update-slice(f32[3,8,8,8,256]{4,2,1,0,3:T(8,128)} %scatter-add.61, f32[3,8,1,8,256]{4,2,1,0,3:T(1,128)S(1)} %fusion.18, s32[]{:T(128)} %constant.397.clone.1, s32[]{:T(128)} %constant.397.clone.1, s32[]{:T(128)} %constant.398.clone.1, s32[]{:T(128)} %constant.397.clone.1, s32[]{:T(128)} %constant.397.clone.1) | dynamic-update-slice | bytes 393220 | tf_op jit(solution)/shard_map/scatter-add | solution.py:33
  224.9 1.7 fusion.17
  227.5 1.8 fusion.26
  229.3 3.5 %copy.90 = f32[3,8,8,8,256]{4,3,2,1,0:T(8,128)} copy(f32[3,8,8,8,256]{4,2,1,0,3:T(8,128)} %fusion.17) | data formatting | bytes 3145728 | tf_op jit(solution)/shard_map/scatter-add | solution.py:37
  233.5 4.0 %scatter-add.66 = f32[3,8,8,8,256]{4,3,2,1,0:T(8,128)} dynamic-update-slice(f32[3,8,8,8,256]{4,3,2,1,0:T(8,128)} %copy.90, f32[2,8,8,1,256]{4,3,2,1,0:T(1,128)S(1)} %fusion.26, s32[]{:T(128)} %constant.399.clone.1, s32[]{:T(128)} %constant.397.clone.1, s32[]{:T(128)} %constant.397.clone.1, s32[]{:T(128)} %constant.397.clone.1, s32[]{:T(128)} %constant.397.clone.1) | dynamic-update-slice | bytes 262148 | tf_op jit(solution)/shard_map/scatter-add | solution.py:38
  237.5 2.1 multiply_add_fusion.1
  239.6 1.2 copy-done.4
  240.9 2.3 scatter-add.69
  243.2 3.9 %multiply_add_fusion = f32[3,8,8,8,256]{4,3,2,1,0:T(8,128)} fusion(f32[3,8,8,8,256]{4,3,2,1,0:T(8,128)} %copy-done.1, f32[3,8,8,8,256]{4,3,2,1,0:T(8,128)} %bitcast.129, f32[3,8,8,8,256]{4,3,2,1,0:T(8,128)} %scatter-add.69), kind=kLoop, calls=%fused_computation.11 | loop fusion | flops 1179648 | bytes 6291456 | tf_op jit(solution)/shard_map/add | solution.py:103
  (62 shorter events, 9.5 us)
Async XLA Ops:
  7.2 47.8 %copy-start = (f32[1,3,512,512]{3,2,1,0:T(8,128)S(1)}, f32[1,3,512,512]{3,2,1,0:T(8,128)}, u32[]{:S(2)}) copy-start(f32[1,3,512,512]{3,2,1,0:T(8,128)} %param.37) | copy-start | bytes 9437188
  7.2 80.2 %reduce-scatter.3.cloned.1.call-start = ((), (), s32[]{:S(2)}) async-start(), calls=%async_computation.4 | async-start | bytes 327680 | tf_op jit(solution)/shard_map/reduce_scatter | solution.py:83
  7.2 9.6 %copy-start.7 = (s32[1,512]{1,0:T(1,128)S(1)}, s32[1,512]{1,0:T(1,128)}, u32[]{:S(2)}) copy-start(s32[1,512]{1,0:T(1,128)} %param.41) | copy-start | bytes 6148
  9.3 1.2 copy-start.5
  11.2 53.5 %collective-permute-start = (f32[3,1,8,8,256]{4,2,1,0,3:T(8,128)}, f32[3,1,8,8,256]{4,2,1,0,3:T(8,128)}, u32[]{:S(2)}, u32[]{:S(2)}) collective-permute-start(f32[3,1,8,8,256]{4,2,1,0,3:T(8,128)} %slice.588), channel_id=1, source_target_pairs={{0,4},{4,8},{8,12},{12,16},{16,20},{20,24},{24,28},{1,5},{5,9},{9,... | collective-permute-start | bytes 589832 | tf_op jit(solution)/shard_map/ppermute | solution.py:17
  64.2 4.2 %copy-start.3 = (f32[1,3,512,256]{3,2,1,0:T(8,128)S(1)}, f32[1,3,512,256]{3,2,1,0:T(8,128)}, u32[]{:S(2)}) copy-start(f32[1,3,512,256]{3,2,1,0:T(8,128)} %param.39) | copy-start | bytes 4718596
  65.8 6.4 %collective-permute-start.1 = (f32[3,1,8,8,256]{4,2,1,0,3:T(8,128)S(1)}, f32[3,1,8,8,256]{4,2,1,0,3:T(8,128)S(1)}, u32[]{:S(2)}, u32[]{:S(2)}) collective-permute-start(f32[3,1,8,8,256]{4,2,1,0,3:T(8,128)S(1)} %get-tuple-element.186), channel_id=1, source_target_pairs={{4,0},{8,4},{12,8},{16,12},{20,16},{24,20},{28,24},{5,1},{9,5},{13... | collective-permute-start | bytes 589832 | tf_op jit(solution)/shard_map/ppermute | solution.py:20
  74.9 17.8 %collective-permute-start.2 = (f32[3,10,1,8,256]{4,2,1,0,3:T(1,128)}, f32[3,10,1,8,256]{4,2,1,0,3:T(1,128)}, u32[]{:S(2)}, u32[]{:S(2)}) collective-permute-start(f32[3,10,1,8,256]{4,2,1,0,3:T(1,128)} %get-tuple-element.181), channel_id=1, source_target_pairs={{0,1},{1,2},{2,3},{4,5},{5,6},{6,7},{8,9},{9,10},{10,11},{12,13},{... | collective-permute-start | bytes 737288 | tf_op jit(solution)/shard_map/ppermute | solution.py:17
  85.5 3.7 %copy-start.8 = (s32[64]{0:T(128)}, s32[64]{0:T(128)S(1)}, u32[]{:S(2)}) copy-start(s32[64]{0:T(128)S(1)} %fusion.36) | copy-start | bytes 772
  85.5 14.0 %collective-permute-start.3 = (f32[3,10,1,8,256]{4,2,1,0,3:T(1,128)}, f32[3,10,1,8,256]{4,2,1,0,3:T(1,128)}, u32[]{:S(2)}, u32[]{:S(2)}) collective-permute-start(f32[3,10,1,8,256]{4,2,1,0,3:T(1,128)} %get-tuple-element.180), channel_id=1, source_target_pairs={{1,0},{2,1},{3,2},{5,4},{6,5},{7,6},{9,8},{10,9},{11,10},{13,12},{... | collective-permute-start | bytes 737288 | tf_op jit(solution)/shard_map/ppermute | solution.py:20
  89.1 32.5 %all-to-all-start = ((f32[8,8,256]{2,1,0:T(8,128)}), f32[8,8,256]{2,1,0:T(8,128)S(1)}, u32[]{:S(2)}, u32[]{:S(2)}) async-start(f32[8,8,256]{2,1,0:T(8,128)} %bitcast.16), calls=%async_computation.1 | async-start | bytes 131072 | tf_op jit(solution)/shard_map/all_to_all | solution.py:92
  92.5 114.6 %reduce-scatter.5.cloned.1.call-start = ((), (), s32[]{:S(2)}) async-start(), calls=%async_computation.5 | async-start | bytes 327680 | tf_op jit(solution)/shard_map/reduce_scatter | solution.py:83
  128.6 1.1 copy-start.1
  129.7 1.2 copy-start.6
  131.6 39.9 %collective-permute-start.4 = (f32[3,1,8,8,256]{4,2,1,0,3:T(8,128)}, f32[3,1,8,8,256]{4,2,1,0,3:T(8,128)}, u32[]{:S(2)}, u32[]{:S(2)}) collective-permute-start(f32[3,1,8,8,256]{4,2,1,0,3:T(8,128)} %slice.605), channel_id=1, source_target_pairs={{0,4},{4,8},{8,12},{12,16},{16,20},{20,24},{24,28},{1,5},{5,9},{9,... | collective-permute-start | bytes 589832 | tf_op jit(solution)/shard_map/ppermute | solution.py:17
  171.4 3.9 %copy-start.2 = (f32[3,8,8,8,256]{4,3,2,1,0:T(8,128)S(1)}, f32[3,8,8,8,256]{4,3,2,1,0:T(8,128)}, u32[]{:S(2)}) copy-start(f32[3,8,8,8,256]{4,3,2,1,0:T(8,128)} %copy-done.1) | copy-start | bytes 4718596
  174.0 6.4 %collective-permute-start.5 = (f32[3,1,8,8,256]{4,2,1,0,3:T(8,128)S(1)}, f32[3,1,8,8,256]{4,2,1,0,3:T(8,128)S(1)}, u32[]{:S(2)}, u32[]{:S(2)}) collective-permute-start(f32[3,1,8,8,256]{4,2,1,0,3:T(8,128)S(1)} %get-tuple-element.184), channel_id=1, source_target_pairs={{4,0},{8,4},{12,8},{16,12},{20,16},{24,20},{28,24},{5,1},{9,5},{13... | collective-permute-start | bytes 589832 | tf_op jit(solution)/shard_map/ppermute | solution.py:20
  183.2 28.9 %collective-permute-start.6 = (f32[3,10,1,8,256]{4,2,1,0,3:T(1,128)}, f32[3,10,1,8,256]{4,2,1,0,3:T(1,128)}, u32[]{:S(2)}, u32[]{:S(2)}) collective-permute-start(f32[3,10,1,8,256]{4,2,1,0,3:T(1,128)} %get-tuple-element.179), channel_id=1, source_target_pairs={{0,1},{1,2},{2,3},{4,5},{5,6},{6,7},{8,9},{9,10},{10,11},{12,13},{... | collective-permute-start | bytes 737288 | tf_op jit(solution)/shard_map/ppermute | solution.py:17
  205.1 13.3 %collective-permute-start.7 = (f32[3,10,1,8,256]{4,2,1,0,3:T(1,128)}, f32[3,10,1,8,256]{4,2,1,0,3:T(1,128)}, u32[]{:S(2)}, u32[]{:S(2)}) collective-permute-start(f32[3,10,1,8,256]{4,2,1,0,3:T(1,128)} %get-tuple-element.178), channel_id=1, source_target_pairs={{1,0},{2,1},{3,2},{5,4},{6,5},{7,6},{9,8},{10,9},{11,10},{13,12},{... | collective-permute-start | bytes 737288 | tf_op jit(solution)/shard_map/ppermute | solution.py:20
  208.8 24.0 %all-to-all-start.1 = ((f32[8,8,256]{2,1,0:T(8,128)}), f32[8,8,256]{2,1,0:T(8,128)S(1)}, u32[]{:S(2)}, u32[]{:S(2)}) async-start(f32[8,8,256]{2,1,0:T(8,128)} %bitcast.26), calls=%async_computation.3 | async-start | bytes 131072 | tf_op jit(solution)/shard_map/all_to_all | solution.py:92
  239.6 1.2 copy-start.4
Sparse Core Ops, SparseCore 0:
  55.0 24.3 reduce-scatter.2
  171.5 24.3 reduce-scatter.4
where the time goes:
time: 256 us; the launch traced here: 254 us
  local copies, waits for them, and re-layouts  77.7 us (30%)
  blocking collectives  56.6 us (22%)
  starting transfers between devices  42.6 us (17%)
  other arithmetic  38.9 us (15%)
  matrix products  15.7 us (6%)
  between operations  14.4 us (6%)
  waiting for transfers between devices  8.06 us (3%)
    all_gather x2, blocking collectives, shards(): gathered = lax.all_gather(top_face, 'surf', axis=0, tiled=True)  56.6 us
    ppermute x4, starting transfers between devices, with_halo(): lax.ppermute(lax.slice_in_dim(block, block.shape[dim] - width, None, axis...  29.2 us
    dot_general x2, matrix products, volume_apply(): applied = jnp.einsum('dab,dbf->daf', kmats, current, precision=highest)  11.9 us
    scatter-add x2, local copies, waits for them, and re-layouts, volume_apply(): extra = extra.at[:, :, 0].add(cube[:, :, 0] - padded[:, 1:-1, 0])  8.99 us
    scatter-add x2, local copies, waits for them, and re-layouts, volume_apply(): extra = extra.at[:, :, -1].add(cube[:, :, -1] - padded[:, 1:-1, -1])  8.99 us
    scatter-add x2, local copies, waits for them, and re-layouts, volume_apply(): extra = extra.at[1:, :, :, 0].add(low_k[1:] - high_k[:-1])  8 us
    ppermute x4, waiting for transfers between devices, with_halo(): lax.ppermute(lax.slice_in_dim(block, 0, width, axis=dim), axis, backward)  7.97 us
    scatter-add x2, local copies, waits for them, and re-layouts, volume_apply(): extra = extra.at[:, :, :, -1].add(high_k - deeper)  6.98 us
  transfers between devices with their start and end apart: 12, of which 2 were waited for; matrix products, arithmetic and copies ran while one was open for 41% of the time, Pallas kernels for 0%

commit v1 on v0

--- a/solution.py
+++ b/solution.py
@@ -75,7 +75,26 @@
     for turn_index in range(ITERS):
         cube = current.reshape(layers_deep, edge_cells, edge_cells, edge_cells, fields)
         top_face = cube[0, :, :, 0, :].reshape(face_nodes, fields)
-        gathered = lax.all_gather(top_face, "surf", axis=0, tiled=True)
+        size, index, rows = (lax.axis_size("surf"), lax.axis_index("surf"), top_face.shape[0])
+        ahead = [(i_2, (i_2 + 1) % size) for i_2 in range(size)]
+        left = [(i_2, (i_2 - 1) % size) for i_2 in range(size)]
+        out = jnp.zeros(
+            (*top_face.shape[:0], size * rows, *top_face.shape[0 + 1 :]), top_face.dtype
+        )
+        out = lax.dynamic_update_slice_in_dim(out, top_face, index * rows, axis=0)
+        from_left = from_right = top_face
+        halfway = size // 2
+        for hop in range(1, halfway + 1):
+            from_left = lax.ppermute(from_left, "surf", ahead)
+            out = lax.dynamic_update_slice_in_dim(
+                out, from_left, (index - hop) % size * rows, axis=0
+            )
+            if hop < size - halfway:
+                from_right = lax.ppermute(from_right, "surf", left)
+                out = lax.dynamic_update_slice_in_dim(
+                    out, from_right, (index + hop) % size * rows, axis=0
+                )
+        gathered = out
         ordered = jnp.take(gathered, group_map, axis=0)
         partial_value = jnp.dot(
             operator_rows, ordered, precision=highest, preferred_element_type=jnp.float32

time: 256 us -> 241 us (0.941)
  blocking collectives: 56.6 us -> 0 us
  local copies, waits for them, and re-layouts: 77.7 us -> 98.3 us
  starting transfers between devices: 42.6 us -> 61.7 us
  other arithmetic: 38.9 us -> 43.2 us
    all_gather x2 -> x0, blocking collectives: 56.6 us -> none  [shards(): gathered = lax.all_gather(top_face, 'surf', axis=0, tiled=True)]
    ppermute x0 -> x14, starting transfers between devices: none -> 28.3 us  [the longest x6 23.5 us: shards(): from_right = lax.ppermute(from_right, 'surf', left)]
    dynamic_update_slice x0 -> x16, local copies, waits for them, and re-layouts: none -> 12.7 us  [the longest x8 6.74 us: shards(): lax.dynamic_update_slice_in_dim(out, from_left, (index - hop) % size * ro...]
    ppermute x4, starting transfers between devices: 29.2 us -> 18.1 us  [with_halo(): lax.ppermute(lax.slice_in_dim(block, block.shape[dim] - width, None, axis...]
    ppermute x4, waiting for transfers between devices: 7.97 us -> 0.01 us  [with_halo(): lax.ppermute(lax.slice_in_dim(block, 0, width, axis=dim), axis, backward)]
    all_to_all x2, waiting for transfers between devices: 0.01 us -> 4.76 us  [shards(): lax.all_to_all(outgoing_back.reshape(surf_count, per_pair, fields), 'surf...]
    slice x2, local copies, waits for them, and re-layouts: 2.19 us -> 6.6 us  [with_halo(): lax.slice_in_dim(block, 0, width, axis=dim)]
    ppermute x0 -> x14, waiting for transfers between devices: none -> 3.23 us  [the longest x8 3.08 us: shards(): from_left = lax.ppermute(from_left, 'surf', ahead)]
  transfers between devices with their start and end apart: 12 -> 26, of which waited for: 2 -> 5; matrix products, arithmetic and copies ran while one was open for 41% -> 51% of each run, Pallas kernels for 0% -> 0%
where the time goes in v1:
time: 241 us; the launch traced here: 239 us
  local copies, waits for them, and re-layouts  98.3 us (41%)
  starting transfers between devices  61.7 us (26%)
  other arithmetic  43.2 us (18%)
  between operations  14.6 us (6%)
  matrix products  13.4 us (6%)
  waiting for transfers between devices  8.04 us (3%)
    ppermute x6, starting transfers between devices, shards(): from_right = lax.ppermute(from_right, 'surf', left)  23.5 us
    ppermute x4, starting transfers between devices, with_halo(): lax.ppermute(lax.slice_in_dim(block, block.shape[dim] - width, None, axis...  18.1 us
    dot_general x2, matrix products, volume_apply(): applied = jnp.einsum('dab,dbf->daf', kmats, current, precision=highest)  11.9 us
    scatter-add x2, local copies, waits for them, and re-layouts, volume_apply(): extra = extra.at[:, :, 0].add(cube[:, :, 0] - padded[:, 1:-1, 0])  9.02 us
    scatter-add x2, local copies, waits for them, and re-layouts, volume_apply(): extra = extra.at[:, :, -1].add(cube[:, :, -1] - padded[:, 1:-1, -1])  9 us
    all_to_all x2, starting transfers between devices, shards(): lax.all_to_all(outgoing_back.reshape(surf_count, per_pair, fields), 'surf...  8.64 us
    scatter-add x2, local copies, waits for them, and re-layouts, volume_apply(): extra = extra.at[1:, :, :, 0].add(low_k[1:] - high_k[:-1])  8.01 us
    scatter-add x2, local copies, waits for them, and re-layouts, volume_apply(): extra = extra.at[:, :, :, -1].add(high_k - deeper)  7.02 us
  transfers between devices with their start and end apart: 26, of which 5 were waited for; matrix products, arithmetic and copies ran while one was open for 51% of the time, Pallas kernels for 0%

profile of v1, /device:TPU:1, one launch (start us, length us, event | category | flops | bytes accessed | tf_op | source)
XLA Modules:
  0.0 239.2 jit_solution(15915059950088302391)
XLA Ops:
  9.1 2.0 collective-permute-start.4
  11.1 3.0 %collective-permute-start.5 = (f32[64,256]{1,0:T(8,128)}, f32[64,256]{1,0:T(8,128)S(1)}, u32[]{:S(2)}, u32[]{:S(2)}) collective-permute-start(f32[64,256]{1,0:T(8,128)} %bitcast.123), channel_id=1, source_target_pairs={{0,28},{4,0},{8,4},{12,8},{16,12},{20,16},{24,20},{28,24},{1,29},{... | collective-permute-start | bytes 196616 | tf_op jit(solution)/shard_map/ppermute | solution.py:93
  14.2 1.9 copy.71
  17.9 2.0 collective-permute-start
  21.4 5.4 %fusion.2 = f32[3,512,256]{2,1,0:T(8,128)} fusion(f32[1,3,512,512]{3,2,1,0:T(8,128)S(1)} %copy-done, f32[1,3,512,256]{3,2,1,0:T(8,128)} %param.39), kind=kOutput, calls=%fused_computation.8 | convolution fusion | flops 2415919104 | bytes 6291456 | tf_op jit(solution)/shard_map/dab,dbf->daf/dot_general | solution.py:39
  28.3 2.0 reshape.729
  30.4 3.8 %sort.17 = (s32[512]{0:T(512)}, s32[512]{0:T(512)S(1)}) sort(s32[512]{0:T(512)S(1)} %bitcast.143, s32[512]{0:T(512)S(1)} %iota.11), dimensions={0}, to_apply=%region_3.5 | sort | flops 4608 | bytes 8192 | tf_op jit(solution)/shard_map/jit(argsort)/sort | solution.py:61
  35.8 3.6 %collective-permute-start.7 = (f32[64,256]{1,0:T(8,128)S(1)}, f32[64,256]{1,0:T(8,128)S(1)}, u32[]{:S(2)}, u32[]{:S(2)}) collective-permute-start(f32[64,256]{1,0:T(8,128)S(1)} %collective-permute-done.5), channel_id=1, source_target_pairs={{0,28},{4,0},{8,4},{12,8},{16,12},{20,16},{24,20},{28,24},{1,29},{... | collective-permute-start | bytes 196616 | tf_op jit(solution)/shard_map/ppermute | solution.py:93
  39.4 1.5 constant_dynamic-update-slice_fusion.20
  41.6 4.2 %collective-permute-start.9 = (f32[64,256]{1,0:T(8,128)S(1)}, f32[64,256]{1,0:T(8,128)S(1)}, u32[]{:S(2)}, u32[]{:S(2)}) collective-permute-start(f32[64,256]{1,0:T(8,128)S(1)} %collective-permute-done.7), channel_id=1, source_target_pairs={{0,28},{4,0},{8,4},{12,8},{16,12},{20,16},{24,20},{28,24},{1,29},{... | collective-permute-start | bytes 196616 | tf_op jit(solution)/shard_map/ppermute | solution.py:93
  48.8 1.8 fusion.44
  52.3 1.5 scatter-add.46
  54.7 3.3 %gather_fusion = f32[512,256]{1,0:T(8,128)} fusion(f32[512,256]{1,0:T(8,128)} %constant_dynamic-update-slice_fusion.14, s32[1024]{0:T(1024)S(1)} %pad_clamp_fusion.1), kind=kCustom, calls=%fused_computation.clone | custom fusion | bytes 1050624 | tf_op jit(solution)/shard_map/jit(_take)/gather | solution.py:98
  58.0 1.8 constant_dynamic-update-slice_fusion
  59.8 3.3 %fusion.41 = (f32[3,10,1,8,256]{4,2,1,0,3:T(1,128)}, f32[3,10,1,8,256]{4,2,1,0,3:T(1,128)}) fusion(f32[3,10,8,8,256]{4,2,1,0,3:T(8,128)} %get-tuple-element.192), kind=kLoop, calls=%fused_computation.125 | loop fusion | bytes 983040 | tf_op jit(solution)/shard_map/slice | solution.py:20
  63.1 6.5 %collective-permute-start.2 = (f32[3,10,1,8,256]{4,2,1,0,3:T(1,128)}, f32[3,10,1,8,256]{4,2,1,0,3:T(1,128)}, u32[]{:S(2)}, u32[]{:S(2)}) collective-permute-start(f32[3,10,1,8,256]{4,2,1,0,3:T(1,128)} %get-tuple-element.181), channel_id=1, source_target_pairs={{0,1},{1,2},{2,3},{4,5},{5,6},{6,7},{8,9},{9,10},{10,11},{12,13},{... | collective-permute-start | bytes 737288 | tf_op jit(solution)/shard_map/ppermute | solution.py:17
  71.2 1.7 copy.79
  72.9 2.1 collective-permute-start.3
  75.1 2.3 fusion.25
  77.3 4.5 %scatter-add.50 = f32[3,8,8,8,256]{4,2,1,0,3:T(8,128)} dynamic-update-slice(f32[3,8,8,8,256]{4,2,1,0,3:T(8,128)} %get-tuple-element.193, f32[3,8,1,8,256]{4,2,1,0,3:T(1,128)S(1)} %fusion.25, s32[]{:T(128)} %constant.454.clone.1, s32[]{:T(128)} %constant.454.clone.1, s32[]{:T(128)} %constant.454.clone.1, s32[]{:T(128)} %constant.454.clone.1, s32[]{:T(128)} %constant.454.clone.1) | dynamic-update-slice | bytes 393220 | tf_op jit(solution)/shard_map/scatter-add | solution.py:32
  81.8 2.4 fusion.24
  84.2 4.5 %scatter-add.51 = f32[3,8,8,8,256]{4,2,1,0,3:T(8,128)} dynamic-update-slice(f32[3,8,8,8,256]{4,2,1,0,3:T(8,128)} %scatter-add.50, f32[3,8,1,8,256]{4,2,1,0,3:T(1,128)S(1)} %fusion.24, s32[]{:T(128)} %constant.454.clone.1, s32[]{:T(128)} %constant.454.clone.1, s32[]{:T(128)} %constant.455.clone.1, s32[]{:T(128)} %constant.454.clone.1, s32[]{:T(128)} %constant.454.clone.1) | dynamic-update-slice | bytes 393220 | tf_op jit(solution)/shard_map/scatter-add | solution.py:33
  88.7 1.8 fusion.23
  90.5 3.5 %copy.78 = f32[3,8,8,8,256]{4,3,2,1,0:T(8,128)} copy(f32[3,8,8,8,256]{4,2,1,0,3:T(8,128)} %fusion.23) | data formatting | bytes 3145728 | tf_op jit(solution)/shard_map/scatter-add | solution.py:37
  94.9 1.8 fusion.27
  96.7 4.0 %scatter-add.55 = f32[3,8,8,8,256]{4,3,2,1,0:T(8,128)} dynamic-update-slice(f32[3,8,8,8,256]{4,3,2,1,0:T(8,128)} %copy.78, f32[2,8,8,1,256]{4,3,2,1,0:T(1,128)S(1)} %fusion.27, s32[]{:T(128)} %constant.456.clone.1, s32[]{:T(128)} %constant.454.clone.1, s32[]{:T(128)} %constant.454.clone.1, s32[]{:T(128)} %constant.454.clone.1, s32[]{:T(128)} %constant.454.clone.1) | dynamic-update-slice | bytes 262148 | tf_op jit(solution)/shard_map/scatter-add | solution.py:38
  100.7 1.7 scatter_custom_fusion
  102.4 5.3 %all-to-all-start = ((f32[8,8,256]{2,1,0:T(8,128)}), f32[8,8,256]{2,1,0:T(8,128)S(1)}, u32[]{:S(2)}, u32[]{:S(2)}) async-start(f32[8,8,256]{2,1,0:T(8,128)} %bitcast.16), calls=%async_computation.1 | async-start | bytes 131072 | tf_op jit(solution)/shard_map/all_to_all | solution.py:111
  107.7 3.3 %multiply_add_fusion.3 = f32[3,8,8,8,256]{4,3,2,1,0:T(8,128)} fusion(f32[3,8,8,8,256]{4,3,2,1,0:T(8,128)} %bitcast.134, f32[3,8,8,8,256]{4,3,2,1,0:T(8,128)} %scatter-add.55), kind=kLoop, calls=%fused_computation.14 | loop fusion | flops 786432 | bytes 4718592 | tf_op jit(solution)/shard_map/add | solution.py:40
  111.0 2.4 %all-to-all-done = f32[8,8,256]{2,1,0:T(8,128)S(1)} async-done(((f32[8,8,256]{2,1,0:T(8,128)}), f32[8,8,256]{2,1,0:T(8,128)S(1)}, u32[]{:S(2)}, u32[]{:S(2)}) %all-to-all-start) | async-done | bytes 65568 | tf_op jit(solution)/shard_map/all_to_all | solution.py:111
  115.3 2.3 scatter-add.56
  117.6 2.8 %multiply_add_fusion.2 = f32[3,8,8,8,256]{4,3,2,1,0:T(8,128)S(1)} fusion(f32[3,8,8,8,256]{4,3,2,1,0:T(8,128)} %bitcast.129, f32[3,8,8,8,256]{4,3,2,1,0:T(8,128)} %bitcast.132, f32[3,8,8,8,256]{4,3,2,1,0:T(8,128)} %scatter-add.56), kind=kLoop, calls=%fused_computation.13 | loop fusion | flops 1179648 | bytes 6291456 | tf_op jit(solution)/shard_map/add | solution.py:122
  121.3 4.1 %collective-permute-start.16 = (f32[64,256]{1,0:T(8,128)}, f32[64,256]{1,0:T(8,128)}, u32[]{:S(2)}, u32[]{:S(2)}) collective-permute-start(f32[64,256]{1,0:T(8,128)} %bitcast.122), channel_id=1, source_target_pairs={{0,28},{4,0},{8,4},{12,8},{16,12},{20,16},{24,20},{28,24},{1,29},{... | collective-permute-start | bytes 196616 | tf_op jit(solution)/shard_map/ppermute | solution.py:93
  126.2 6.5 %fusion.5 = f32[3,512,256]{1,2,0:T(8,128)} fusion(f32[3,512,256]{2,1,0:T(8,128)S(1)} %bitcast.124, f32[1,3,512,512]{3,2,1,0:T(8,128)S(1)} %copy-done), kind=kOutput, calls=%fused_computation.15 | convolution fusion | flops 2415919104 | bytes 6291456 | tf_op jit(solution)/shard_map/dab,dbf->daf/dot_general | solution.py:39
  137.9 3.0 %copy.82 = f32[3,512,256]{2,1,0:T(8,128)} copy(f32[3,512,256]{1,2,0:T(8,128)} %fusion.5) | data formatting | bytes 3145728 | tf_op jit(solution)/shard_map/dab,dbf->daf/dot_general | solution.py:39
  141.0 1.5 constant_dynamic-update-slice_fusion.12
  142.5 4.2 %collective-permute-start.18 = (f32[64,256]{1,0:T(8,128)}, f32[64,256]{1,0:T(8,128)S(1)}, u32[]{:S(2)}, u32[]{:S(2)}) collective-permute-start(f32[64,256]{1,0:T(8,128)} %collective-permute-done.16), channel_id=1, source_target_pairs={{0,28},{4,0},{8,4},{12,8},{16,12},{20,16},{24,20},{28,24},{1,29},{... | collective-permute-start | bytes 196616 | tf_op jit(solution)/shard_map/ppermute | solution.py:93
  146.6 1.5 constant_dynamic-update-slice_fusion.11
  148.3 4.5 %collective-permute-start.20 = (f32[64,256]{1,0:T(8,128)S(1)}, f32[64,256]{1,0:T(8,128)S(1)}, u32[]{:S(2)}, u32[]{:S(2)}) collective-permute-start(f32[64,256]{1,0:T(8,128)S(1)} %collective-permute-done.18), channel_id=1, source_target_pairs={{0,28},{4,0},{8,4},{12,8},{16,12},{20,16},{24,20},{28,24},{1,29},{... | collective-permute-start | bytes 196616 | tf_op jit(solution)/shard_map/ppermute | solution.py:93
  154.0 1.7 fusion.43
  155.7 1.9 constant_dynamic-update-slice_fusion.4
  158.9 1.3 scatter-add.59
  160.2 2.1 collective-permute-start.21
  163.6 2.6 %collective-permute-done.21 = f32[64,256]{1,0:T(8,128)S(1)} collective-permute-done((f32[64,256]{1,0:T(8,128)S(1)}, f32[64,256]{1,0:T(8,128)S(1)}, u32[]{:S(2)}, u32[]{:S(2)}) %collective-permute-start.21) | collective-permute-done | bytes 65568 | tf_op jit(solution)/shard_map/ppermute | solution.py:88
  166.8 3.3 %gather_fusion.2 = f32[512,256]{1,0:T(8,128)} fusion(f32[512,256]{1,0:T(8,128)} %constant_dynamic-update-slice_fusion.6, s32[1024]{0:T(1024)S(1)} %pad_clamp_fusion.1), kind=kCustom, calls=%fused_computation.2.clone | custom fusion | bytes 1050624 | tf_op jit(solution)/shard_map/jit(_take)/gather | solution.py:98
  170.0 1.8 constant_dynamic-update-slice_fusion.3
  171.9 3.3 %fusion.40 = (f32[3,10,1,8,256]{4,2,1,0,3:T(1,128)}, f32[3,10,1,8,256]{4,2,1,0,3:T(1,128)}) fusion(f32[3,10,8,8,256]{4,2,1,0,3:T(8,128)} %get-tuple-element.190), kind=kLoop, calls=%fused_computation.124 | loop fusion | bytes 983040 | tf_op jit(solution)/shard_map/slice | solution.py:20
  175.2 8.3 %collective-permute-start.13 = (f32[3,10,1,8,256]{4,2,1,0,3:T(1,128)}, f32[3,10,1,8,256]{4,2,1,0,3:T(1,128)}, u32[]{:S(2)}, u32[]{:S(2)}) collective-permute-start(f32[3,10,1,8,256]{4,2,1,0,3:T(1,128)} %get-tuple-element.179), channel_id=1, source_target_pairs={{0,1},{1,2},{2,3},{4,5},{5,6},{6,7},{8,9},{9,10},{10,11},{12,13},{... | collective-permute-start | bytes 737288 | tf_op jit(solution)/shard_map/ppermute | solution.py:17
  185.0 1.7 copy.91
  186.8 1.9 collective-permute-start.14
  188.7 1.9 fusion.19
  190.6 4.5 %scatter-add.61 = f32[3,8,8,8,256]{4,2,1,0,3:T(8,128)} dynamic-update-slice(f32[3,8,8,8,256]{4,2,1,0,3:T(8,128)} %get-tuple-element.191, f32[3,8,1,8,256]{4,2,1,0,3:T(1,128)S(1)} %fusion.19, s32[]{:T(128)} %constant.454.clone.1, s32[]{:T(128)} %constant.454.clone.1, s32[]{:T(128)} %constant.454.clone.1, s32[]{:T(128)} %constant.454.clone.1, s32[]{:T(128)} %constant.454.clone.1) | dynamic-update-slice | bytes 393220 | tf_op jit(solution)/shard_map/scatter-add | solution.py:32
  195.1 1.9 fusion.18
  197.0 4.5 %scatter-add.64 = f32[3,8,8,8,256]{4,2,1,0,3:T(8,128)} dynamic-update-slice(f32[3,8,8,8,256]{4,2,1,0,3:T(8,128)} %scatter-add.61, f32[3,8,1,8,256]{4,2,1,0,3:T(1,128)S(1)} %fusion.18, s32[]{:T(128)} %constant.454.clone.1, s32[]{:T(128)} %constant.454.clone.1, s32[]{:T(128)} %constant.455.clone.1, s32[]{:T(128)} %constant.454.clone.1, s32[]{:T(128)} %constant.454.clone.1) | dynamic-update-slice | bytes 393220 | tf_op jit(solution)/shard_map/scatter-add | solution.py:33
  201.5 1.8 fusion.17
  204.2 3.5 %copy.90 = f32[3,8,8,8,256]{4,3,2,1,0:T(8,128)} copy(f32[3,8,8,8,256]{4,2,1,0,3:T(8,128)} %fusion.17) | data formatting | bytes 3145728 | tf_op jit(solution)/shard_map/scatter-add | solution.py:37
  207.7 1.8 fusion.26
  209.5 4.0 %scatter-add.66 = f32[3,8,8,8,256]{4,3,2,1,0:T(8,128)} dynamic-update-slice(f32[3,8,8,8,256]{4,3,2,1,0:T(8,128)} %copy.90, f32[2,8,8,1,256]{4,3,2,1,0:T(1,128)S(1)} %fusion.26, s32[]{:T(128)} %constant.456.clone.1, s32[]{:T(128)} %constant.454.clone.1, s32[]{:T(128)} %constant.454.clone.1, s32[]{:T(128)} %constant.454.clone.1, s32[]{:T(128)} %constant.454.clone.1) | dynamic-update-slice | bytes 262148 | tf_op jit(solution)/shard_map/scatter-add | solution.py:38
  213.5 1.7 scatter_custom_fusion.1
  215.2 3.3 %all-to-all-start.1 = ((f32[8,8,256]{2,1,0:T(8,128)}), f32[8,8,256]{2,1,0:T(8,128)S(1)}, u32[]{:S(2)}, u32[]{:S(2)}) async-start(f32[8,8,256]{2,1,0:T(8,128)} %bitcast.26), calls=%async_computation.3 | async-start | bytes 131072 | tf_op jit(solution)/shard_map/all_to_all | solution.py:111
  218.6 3.3 %multiply_add_fusion.1 = f32[3,8,8,8,256]{4,3,2,1,0:T(8,128)} fusion(f32[3,8,8,8,256]{4,3,2,1,0:T(8,128)} %bitcast.131, f32[3,8,8,8,256]{4,3,2,1,0:T(8,128)} %scatter-add.66), kind=kLoop, calls=%fused_computation.12 | loop fusion | flops 786432 | bytes 4718592 | tf_op jit(solution)/shard_map/add | solution.py:40
  221.9 2.3 all-to-all-done.1
  226.1 2.3 scatter-add.69
  228.5 3.9 %multiply_add_fusion = f32[3,8,8,8,256]{4,3,2,1,0:T(8,128)} fusion(f32[3,8,8,8,256]{4,3,2,1,0:T(8,128)} %copy-done.1, f32[3,8,8,8,256]{4,3,2,1,0:T(8,128)} %bitcast.133, f32[3,8,8,8,256]{4,3,2,1,0:T(8,128)} %scatter-add.69), kind=kLoop, calls=%fused_computation.11 | loop fusion | flops 1179648 | bytes 6291456 | tf_op jit(solution)/shard_map/add | solution.py:122
  (114 shorter events, 34.7 us)
Async XLA Ops:
  7.2 14.2 %copy-start = (f32[1,3,512,512]{3,2,1,0:T(8,128)S(1)}, f32[1,3,512,512]{3,2,1,0:T(8,128)}, u32[]{:S(2)}) copy-start(f32[1,3,512,512]{3,2,1,0:T(8,128)} %param.37) | copy-start | bytes 9437188
  7.2 93.5 %reduce-scatter.3.cloned.1.call-start = ((), (), s32[]{:S(2)}) async-start(), calls=%async_computation.4 | async-start | bytes 327680 | tf_op jit(solution)/shard_map/reduce_scatter | solution.py:102
  9.1 12.2 %copy-start.12 = (s32[1,512]{1,0:T(1,128)S(1)}, s32[1,512]{1,0:T(1,128)}, u32[]{:S(2)}) copy-start(s32[1,512]{1,0:T(1,128)} %param.41) | copy-start | bytes 6148
  9.1 26.1 %collective-permute-start.4 = (f32[64,256]{1,0:T(8,128)}, f32[64,256]{1,0:T(8,128)}, u32[]{:S(2)}, u32[]{:S(2)}) collective-permute-start(f32[64,256]{1,0:T(8,128)} %bitcast.123), channel_id=1, source_target_pairs={{0,4},{4,8},{8,12},{12,16},{16,20},{20,24},{24,28},{28,0},{1,5},{5... | collective-permute-start | bytes 196616 | tf_op jit(solution)/shard_map/ppermute | solution.py:88
  11.1 24.7 %collective-permute-start.5 = (f32[64,256]{1,0:T(8,128)}, f32[64,256]{1,0:T(8,128)S(1)}, u32[]{:S(2)}, u32[]{:S(2)}) collective-permute-start(f32[64,256]{1,0:T(8,128)} %bitcast.123), channel_id=1, source_target_pairs={{0,28},{4,0},{8,4},{12,8},{16,12},{20,16},{24,20},{28,24},{1,29},{... | collective-permute-start | bytes 196616 | tf_op jit(solution)/shard_map/ppermute | solution.py:93
  16.1 1.1 copy-start.3
  17.9 30.8 %collective-permute-start = (f32[3,1,8,8,256]{4,2,1,0,3:T(8,128)}, f32[3,1,8,8,256]{4,2,1,0,3:T(8,128)}, u32[]{:S(2)}, u32[]{:S(2)}) collective-permute-start(f32[3,1,8,8,256]{4,2,1,0,3:T(8,128)} %slice.588), channel_id=1, source_target_pairs={{0,4},{4,8},{8,12},{12,16},{16,20},{20,24},{24,28},{1,5},{5,9},{9,... | collective-permute-start | bytes 589832 | tf_op jit(solution)/shard_map/ppermute | solution.py:17
  35.2 16.7 %copy-start.2 = (f32[1,3,512,256]{3,2,1,0:T(8,128)S(1)}, f32[1,3,512,256]{3,2,1,0:T(8,128)}, u32[]{:S(2)}) copy-start(f32[1,3,512,256]{3,2,1,0:T(8,128)} %param.39) | copy-start | bytes 4718596
  35.2 6.3 %collective-permute-start.6 = (f32[64,256]{1,0:T(8,128)}, f32[64,256]{1,0:T(8,128)S(1)}, u32[]{:S(2)}, u32[]{:S(2)}) collective-permute-start(f32[64,256]{1,0:T(8,128)} %collective-permute-done.4), channel_id=1, source_target_pairs={{0,4},{4,8},{8,12},{12,16},{16,20},{20,24},{24,28},{28,0},{1,5},{5... | collective-permute-start | bytes 196616 | tf_op jit(solution)/shard_map/ppermute | solution.py:88
  35.8 5.7 %collective-permute-start.7 = (f32[64,256]{1,0:T(8,128)S(1)}, f32[64,256]{1,0:T(8,128)S(1)}, u32[]{:S(2)}, u32[]{:S(2)}) collective-permute-start(f32[64,256]{1,0:T(8,128)S(1)} %collective-permute-done.5), channel_id=1, source_target_pairs={{0,28},{4,0},{8,4},{12,8},{16,12},{20,16},{24,20},{28,24},{1,29},{... | collective-permute-start | bytes 196616 | tf_op jit(solution)/shard_map/ppermute | solution.py:93
  41.6 5.9 %collective-permute-start.8 = (f32[64,256]{1,0:T(8,128)S(1)}, f32[64,256]{1,0:T(8,128)S(1)}, u32[]{:S(2)}, u32[]{:S(2)}) collective-permute-start(f32[64,256]{1,0:T(8,128)S(1)} %collective-permute-done.6), channel_id=1, source_target_pairs={{0,4},{4,8},{8,12},{12,16},{16,20},{20,24},{24,28},{28,0},{1,5},{5... | collective-permute-start | bytes 196616 | tf_op jit(solution)/shard_map/ppermute | solution.py:88
  41.6 6.5 %collective-permute-start.9 = (f32[64,256]{1,0:T(8,128)S(1)}, f32[64,256]{1,0:T(8,128)S(1)}, u32[]{:S(2)}, u32[]{:S(2)}) collective-permute-start(f32[64,256]{1,0:T(8,128)S(1)} %collective-permute-done.7), channel_id=1, source_target_pairs={{0,28},{4,0},{8,4},{12,8},{16,12},{20,16},{24,20},{28,24},{1,29},{... | collective-permute-start | bytes 196616 | tf_op jit(solution)/shard_map/ppermute | solution.py:93
  47.5 6.6 %collective-permute-start.10 = (f32[64,256]{1,0:T(8,128)S(1)}, f32[64,256]{1,0:T(8,128)S(1)}, u32[]{:S(2)}, u32[]{:S(2)}) collective-permute-start(f32[64,256]{1,0:T(8,128)S(1)} %collective-permute-done.8), channel_id=1, source_target_pairs={{0,4},{4,8},{8,12},{12,16},{16,20},{20,24},{24,28},{28,0},{1,5},{5... | collective-permute-start | bytes 196616 | tf_op jit(solution)/shard_map/ppermute | solution.py:88
  50.5 7.5 %collective-permute-start.1 = (f32[3,1,8,8,256]{4,2,1,0,3:T(8,128)}, f32[3,1,8,8,256]{4,2,1,0,3:T(8,128)S(1)}, u32[]{:S(2)}, u32[]{:S(2)}) collective-permute-start(f32[3,1,8,8,256]{4,2,1,0,3:T(8,128)} %get-tuple-element.186), channel_id=1, source_target_pairs={{4,0},{8,4},{12,8},{16,12},{20,16},{24,20},{28,24},{5,1},{9,5},{13... | collective-permute-start | bytes 589832 | tf_op jit(solution)/shard_map/ppermute | solution.py:20
  52.3 1.8 copy-start.10
  58.0 11.6 %copy-start.4 = (f32[256,512]{1,0:T(8,128)S(1)}, f32[256,512]{1,0:T(8,128)}, u32[]{:S(2)}) copy-start(f32[256,512]{1,0:T(8,128)} %reshape.729) | copy-start | bytes 1572868
  58.0 11.7 %copy-start.8 = (f32[512,256]{1,0:T(8,128)S(1)}, f32[512,256]{1,0:T(8,128)}, u32[]{:S(2)}) copy-start(f32[512,256]{1,0:T(8,128)} %gather_fusion) | copy-start | bytes 1572868
  63.1 11.9 %collective-permute-start.2 = (f32[3,10,1,8,256]{4,2,1,0,3:T(1,128)}, f32[3,10,1,8,256]{4,2,1,0,3:T(1,128)}, u32[]{:S(2)}, u32[]{:S(2)}) collective-permute-start(f32[3,10,1,8,256]{4,2,1,0,3:T(1,128)} %get-tuple-element.181), channel_id=1, source_target_pairs={{0,1},{1,2},{2,3},{4,5},{5,6},{6,7},{8,9},{9,10},{10,11},{12,13},{... | collective-permute-start | bytes 737288 | tf_op jit(solution)/shard_map/ppermute | solution.py:17
  72.9 8.9 %collective-permute-start.3 = (f32[3,10,1,8,256]{4,2,1,0,3:T(1,128)}, f32[3,10,1,8,256]{4,2,1,0,3:T(1,128)}, u32[]{:S(2)}, u32[]{:S(2)}) collective-permute-start(f32[3,10,1,8,256]{4,2,1,0,3:T(1,128)} %get-tuple-element.180), channel_id=1, source_target_pairs={{1,0},{2,1},{3,2},{5,4},{6,5},{7,6},{9,8},{10,9},{11,10},{13,12},{... | collective-permute-start | bytes 737288 | tf_op jit(solution)/shard_map/ppermute | solution.py:20
  102.4 11.0 %all-to-all-start = ((f32[8,8,256]{2,1,0:T(8,128)}), f32[8,8,256]{2,1,0:T(8,128)S(1)}, u32[]{:S(2)}, u32[]{:S(2)}) async-start(f32[8,8,256]{2,1,0:T(8,128)} %bitcast.16), calls=%async_computation.1 | async-start | bytes 131072 | tf_op jit(solution)/shard_map/all_to_all | solution.py:111
  107.7 105.9 %reduce-scatter.5.cloned.1.call-start = ((), (), s32[]{:S(2)}) async-start(), calls=%async_computation.5 | async-start | bytes 327680 | tf_op jit(solution)/shard_map/reduce_scatter | solution.py:102
  120.4 14.4 %copy-start.1 = (f32[3,8,8,8,256]{4,3,2,1,0:T(8,128)}, f32[3,8,8,8,256]{4,3,2,1,0:T(8,128)S(1)}, u32[]{:S(2)}) copy-start(f32[3,8,8,8,256]{4,3,2,1,0:T(8,128)S(1)} %multiply_add_fusion.2) | copy-start | bytes 4718596
  121.2 19.8 %collective-permute-start.15 = (f32[64,256]{1,0:T(8,128)}, f32[64,256]{1,0:T(8,128)}, u32[]{:S(2)}, u32[]{:S(2)}) collective-permute-start(f32[64,256]{1,0:T(8,128)} %bitcast.122), channel_id=1, source_target_pairs={{0,4},{4,8},{8,12},{12,16},{16,20},{20,24},{24,28},{28,0},{1,5},{5... | collective-permute-start | bytes 196616 | tf_op jit(solution)/shard_map/ppermute | solution.py:88
  121.3 21.2 %collective-permute-start.16 = (f32[64,256]{1,0:T(8,128)}, f32[64,256]{1,0:T(8,128)}, u32[]{:S(2)}, u32[]{:S(2)}) collective-permute-start(f32[64,256]{1,0:T(8,128)} %bitcast.122), channel_id=1, source_target_pairs={{0,28},{4,0},{8,4},{12,8},{16,12},{20,16},{24,20},{28,24},{1,29},{... | collective-permute-start | bytes 196616 | tf_op jit(solution)/shard_map/ppermute | solution.py:93
  134.8 1.2 copy-start.6
  136.0 18.0 %collective-permute-start.11 = (f32[3,1,8,8,256]{4,2,1,0,3:T(8,128)S(1)}, f32[3,1,8,8,256]{4,2,1,0,3:T(8,128)S(1)}, u32[]{:S(2)}, u32[]{:S(2)}) collective-permute-start(f32[3,1,8,8,256]{4,2,1,0,3:T(8,128)S(1)} %slice.605), channel_id=1, source_target_pairs={{0,4},{4,8},{8,12},{12,16},{16,20},{20,24},{24,28},{1,5},{5,9},{9,... | collective-permute-start | bytes 589832 | tf_op jit(solution)/shard_map/ppermute | solution.py:17
  141.0 7.2 %collective-permute-start.17 = (f32[64,256]{1,0:T(8,128)}, f32[64,256]{1,0:T(8,128)S(1)}, u32[]{:S(2)}, u32[]{:S(2)}) collective-permute-start(f32[64,256]{1,0:T(8,128)} %collective-permute-done.15), channel_id=1, source_target_pairs={{0,4},{4,8},{8,12},{12,16},{16,20},{20,24},{24,28},{28,0},{1,5},{5... | collective-permute-start | bytes 196616 | tf_op jit(solution)/shard_map/ppermute | solution.py:88
  142.5 5.8 %collective-permute-start.18 = (f32[64,256]{1,0:T(8,128)}, f32[64,256]{1,0:T(8,128)S(1)}, u32[]{:S(2)}, u32[]{:S(2)}) collective-permute-start(f32[64,256]{1,0:T(8,128)} %collective-permute-done.16), channel_id=1, source_target_pairs={{0,28},{4,0},{8,4},{12,8},{16,12},{20,16},{24,20},{28,24},{1,29},{... | collective-permute-start | bytes 196616 | tf_op jit(solution)/shard_map/ppermute | solution.py:93
  148.1 12.1 %collective-permute-start.19 = (f32[64,256]{1,0:T(8,128)S(1)}, f32[64,256]{1,0:T(8,128)S(1)}, u32[]{:S(2)}, u32[]{:S(2)}) collective-permute-start(f32[64,256]{1,0:T(8,128)S(1)} %collective-permute-done.17), channel_id=1, source_target_pairs={{0,4},{4,8},{8,12},{12,16},{16,20},{20,24},{24,28},{28,0},{1,5},{5... | collective-permute-start | bytes 196616 | tf_op jit(solution)/shard_map/ppermute | solution.py:88
  148.3 14.7 %collective-permute-start.20 = (f32[64,256]{1,0:T(8,128)S(1)}, f32[64,256]{1,0:T(8,128)S(1)}, u32[]{:S(2)}, u32[]{:S(2)}) collective-permute-start(f32[64,256]{1,0:T(8,128)S(1)} %collective-permute-done.18), channel_id=1, source_target_pairs={{0,28},{4,0},{8,4},{12,8},{16,12},{20,16},{24,20},{28,24},{1,29},{... | collective-permute-start | bytes 196616 | tf_op jit(solution)/shard_map/ppermute | solution.py:93
  157.6 2.7 %copy-start.11 = (f32[3,10,8,8,256]{4,2,1,0,3:T(8,128)}, f32[3,10,8,8,256]{4,2,1,0,3:T(8,128)S(1)}, u32[]{:S(2)}) copy-start(f32[3,10,8,8,256]{4,2,1,0,3:T(8,128)S(1)} %constant_dynamic-update-slice_fusion.4) | copy-start | bytes 5898244
  157.6 12.5 %collective-permute-start.12 = (f32[3,1,8,8,256]{4,2,1,0,3:T(8,128)}, f32[3,1,8,8,256]{4,2,1,0,3:T(8,128)S(1)}, u32[]{:S(2)}, u32[]{:S(2)}) collective-permute-start(f32[3,1,8,8,256]{4,2,1,0,3:T(8,128)} %get-tuple-element.184), channel_id=1, source_target_pairs={{4,0},{8,4},{12,8},{16,12},{20,16},{24,20},{28,24},{5,1},{9,5},{13... | collective-permute-start | bytes 589832 | tf_op jit(solution)/shard_map/ppermute | solution.py:20
  160.2 5.9 %collective-permute-start.21 = (f32[64,256]{1,0:T(8,128)S(1)}, f32[64,256]{1,0:T(8,128)S(1)}, u32[]{:S(2)}, u32[]{:S(2)}) collective-permute-start(f32[64,256]{1,0:T(8,128)S(1)} %collective-permute-done.19), channel_id=1, source_target_pairs={{0,4},{4,8},{8,12},{12,16},{16,20},{20,24},{24,28},{28,0},{1,5},{5... | collective-permute-start | bytes 196616 | tf_op jit(solution)/shard_map/ppermute | solution.py:88
  170.0 13.5 %copy-start.5 = (f32[256,512]{1,0:T(8,128)S(1)}, f32[256,512]{1,0:T(8,128)}, u32[]{:S(2)}) copy-start(f32[256,512]{1,0:T(8,128)} %reshape.729) | copy-start | bytes 1572868
  170.0 13.5 %copy-start.7 = (f32[512,256]{1,0:T(8,128)S(1)}, f32[512,256]{1,0:T(8,128)}, u32[]{:S(2)}) copy-start(f32[512,256]{1,0:T(8,128)} %gather_fusion.2) | copy-start | bytes 1572868
  175.2 13.5 %collective-permute-start.13 = (f32[3,10,1,8,256]{4,2,1,0,3:T(1,128)}, f32[3,10,1,8,256]{4,2,1,0,3:T(1,128)}, u32[]{:S(2)}, u32[]{:S(2)}) collective-permute-start(f32[3,10,1,8,256]{4,2,1,0,3:T(1,128)} %get-tuple-element.179), channel_id=1, source_target_pairs={{0,1},{1,2},{2,3},{4,5},{5,6},{6,7},{8,9},{9,10},{10,11},{12,13},{... | collective-permute-start | bytes 737288 | tf_op jit(solution)/shard_map/ppermute | solution.py:17
  185.0 10.1 %copy-start.9 = (f32[3,8,1,8,256]{4,3,2,1,0:T(8,128)S(1)}, f32[3,8,1,8,256]{4,3,2,1,0:T(8,128)}, u32[]{:S(2)}) copy-start(f32[3,8,1,8,256]{4,3,2,1,0:T(8,128)} %get-tuple-element.182) | copy-start | bytes 589828
  186.8 8.3 %collective-permute-start.14 = (f32[3,10,1,8,256]{4,2,1,0,3:T(1,128)}, f32[3,10,1,8,256]{4,2,1,0,3:T(1,128)}, u32[]{:S(2)}, u32[]{:S(2)}) collective-permute-start(f32[3,10,1,8,256]{4,2,1,0,3:T(1,128)} %get-tuple-element.178), channel_id=1, source_target_pairs={{1,0},{2,1},{3,2},{5,4},{6,5},{7,6},{9,8},{10,9},{11,10},{13,12},{... | collective-permute-start | bytes 737288 | tf_op jit(solution)/shard_map/ppermute | solution.py:20
  215.2 9.0 %all-to-all-start.1 = ((f32[8,8,256]{2,1,0:T(8,128)}), f32[8,8,256]{2,1,0:T(8,128)S(1)}, u32[]{:S(2)}, u32[]{:S(2)}) async-start(f32[8,8,256]{2,1,0:T(8,128)} %bitcast.26), calls=%async_computation.3 | async-start | bytes 131072 | tf_op jit(solution)/shard_map/all_to_all | solution.py:111
Sparse Core Ops, SparseCore 0:
  73.1 19.3 reduce-scatter.2
  186.9 15.4 reduce-scatter.4
